TPU v7x, 32 devices: a whole 2x2x4 slice. The times are simulated.
32 devices in a mesh: batch: 4 (over x, core), centers: 8 (over z, y).
Axes of the slice: x: 2, y: 2, z: 4, core: 2. Of those that a mesh axis runs over, the one named last changes fastest.
Arguments:
- pool_features: float32 [32768, 128], P(('batch', 'centers')), may hold values from -14 to 14
- pool_targets: float32 [32768, 64], P(('batch', 'centers')), may hold values from -6 to 6
- batch_index: int32 [2048], P(('batch', 'centers')), may hold values from 0 to 1023
- centers: float32 [4096, 128], P('centers'), may hold values from -14 to 14
- weights: float32 [4096, 64], P('centers'), as said below
- eig_vectors: float32 [4096, 1024], P(('batch', 'centers')), may hold values from -0.09375 to 0.09375
- eig_scale: float32 [1024], replicated, may hold values from 0.5 to 4
- nys_owner: int32 [4096, 1], P(('batch', 'centers')), may hold values from 0 to 7; in each aligned block of 128 rows (0 to 127, 128 to 255, ...) at most 32 rows name the same one
- nys_offset: int32 [4096], P(('batch', 'centers')), may hold values from 0 to 511
Outputs:
- residual_out: float32 [2048, 64], P(('batch', 'centers'))
- update: float32 [4096, 64], P('centers')
Inputs may be any that keep to these rules, and one draw needn't show every extreme that they name: `nys_owner`: among the 128 rows of one device no owner is named more than 32 times; on some devices one owner is named exactly 32 times. `weights`: every column sums to zero.
All inputs are finite; a program needn't handle non-finite values.
Results may differ from a plain program's by a relative error of at most 0.0003.
Values sent between devices are 32-bit elements; how exact they have to be, the bound alone decides.
A program may use at most 64 MiB of HBM per device.

v0:
```python
import math
import jax
import jax.numpy as jnp
from jax import lax
from jax.sharding import PartitionSpec as P

DEPTH = 3
epsilon = 1e-06
highest = lax.Precision.HIGHEST


def kernel_rows(row_block, center_block, center_norm):
    inner_prod = (
        lax.dot_general(
            row_block,
            center_block,
            (((1,), (1,)), ((), ())),
            precision=highest,
            preferred_element_type=jnp.float32,
        )
        / row_block.shape[1]
    )
    row_norm = jnp.mean(row_block * row_block, axis=1) + epsilon
    norm_scale = jnp.sqrt(row_norm[:, None] * center_norm[None, :])
    sigma_now = inner_prod
    tangent = inner_prod
    for depth_step in range(DEPTH):
        cosine = sigma_now / norm_scale
        arc_angle = jnp.arccos(cosine)
        remain = (math.pi - arc_angle) / math.pi
        sigma_now = (
            norm_scale
            * (jnp.sqrt(1.0 - cosine * cosine) + (math.pi - arc_angle) * cosine)
            / math.pi
        )
        tangent = sigma_now + tangent * remain
    return tangent


def per_device(
    pool_features,
    pool_targets,
    batch_index,
    centers,
    weights,
    eig_vectors,
    eig_scale,
    nys_owner,
    nys_offset,
):
    local_rows = pool_features[batch_index]
    local_targets = pool_targets[batch_index]
    row_count = local_rows.shape[0]
    group_size = lax.axis_size("centers")
    rows_total = row_count * group_size * lax.axis_size("batch")
    center_count = centers.shape[0]
    outputs = weights.shape[1]
    center_norm = jnp.mean(centers * centers, axis=1) + epsilon
    kernel = kernel_rows(
        lax.all_gather(local_rows, "centers", axis=0, tiled=True), centers, center_norm
    )
    partial_pred = jnp.dot(kernel, weights, precision=highest, preferred_element_type=jnp.float32)
    all_targets = lax.all_gather(local_targets, "centers", axis=0, tiled=True)
    prediction = lax.psum(partial_pred, "centers")
    residual = prediction - all_targets
    own_residual = lax.dynamic_slice_in_dim(
        residual, lax.axis_index("centers") * row_count, row_count, 0
    )
    grads_part = lax.dot_general(
        kernel,
        residual,
        (((0,), (0,)), ((), ())),
        precision=highest,
        preferred_element_type=jnp.float32,
    ) / math.sqrt(rows_total)
    grads = lax.psum(grads_part, "batch")
    owner = nys_owner[:, 0]
    slots = max(2, 2 * owner.shape[0] // group_size)
    owner_hot = (owner[:, None] == jnp.arange(group_size, dtype=jnp.int32)[None, :]).astype(
        jnp.int32
    )
    slot_rank = jnp.sum((jnp.cumsum(owner_hot, axis=0) - owner_hot) * owner_hot, axis=1)
    requests = jnp.zeros((group_size, slots), jnp.int32).at[owner, slot_rank].set(nys_offset)
    received = lax.all_to_all(requests, "centers", split_axis=0, concat_axis=0, tiled=True)
    found = grads[received]
    returned = lax.all_to_all(found, "centers", split_axis=0, concat_axis=0, tiled=True)
    picked_grads = returned[owner, slot_rank]
    coeff_part = lax.dot_general(
        eig_vectors,
        picked_grads,
        (((0,), (0,)), ((), ())),
        precision=highest,
        preferred_element_type=jnp.float32,
    )
    coeff = lax.psum(coeff_part, ("batch", "centers"))
    corr_rows = jnp.dot(
        eig_vectors,
        eig_scale[:, None] * coeff,
        precision=highest,
        preferred_element_type=jnp.float32,
    )
    outgoing = (
        jnp.zeros((group_size, slots, outputs), jnp.float32).at[owner, slot_rank].set(corr_rows)
    )
    incoming = lax.all_to_all(outgoing, "centers", split_axis=0, concat_axis=0, tiled=True)
    corr_part = jnp.zeros((center_count, outputs), jnp.float32).at[received].add(incoming)
    correction = lax.psum(corr_part, "batch")
    return (own_residual, correction - grads)


def solution(mesh):
    placed = (
        P(("batch", "centers"), None),
        P(("batch", "centers"), None),
        P(("batch", "centers")),
        P("centers", None),
        P("centers", None),
        P(("batch", "centers"), None),
        P(),
        P(("batch", "centers"), None),
        P(("batch", "centers")),
    )
    return jax.shard_map(
        per_device,
        mesh=mesh,
        in_specs=placed,
        out_specs=(P(("batch", "centers"), None), P("centers", None)),
        check_vma=False,
    )
```

profile of v0, /device:TPU:0, one launch (start us, length us, event | category | flops | bytes accessed | tf_op | source)
XLA Modules:
  0.0 387.0 jit_solution(5106888059048131326)
XLA Ops:
  7.2 0.7 copy-done.6
  8.4 0.6 broadcast.104
  9.0 19.9 %scatter_fusion = s32[8,32]{1,0:T(8,128)} fusion(s32[8,32]{1,0:T(8,128)} %broadcast.104, s32[128]{0:T(128)S(1)} %get-tuple-element.8, s32[128]{0:T(128)S(1)} %copy-done.8), kind=kCustom, calls=%fused_computation.4 | custom fusion | bytes 2560 | tf_op jit(solution)/shard_map/scatter | solution.py:83
  28.9 7.4 %all-to-all-start = ((s32[8,1,32]{2,1,0:T(1,128)}), s32[8,1,32]{2,1,0:T(1,128)S(1)}, u32[]{:S(2)}, u32[]{:S(2)}) async-start(s32[8,1,32]{2,1,0:T(1,128)} %bitcast.4), calls=%async_computation | async-start | bytes 8192 | tf_op jit(solution)/shard_map/all_to_all | solution.py:84
  36.6 0.6 gather_fusion
  37.2 31.2 %all-gather = f32[512,128]{1,0:T(8,128)S(1)} all-gather(f32[64,128]{1,0:T(8,128)S(1)} %gather_fusion), channel_id=2, replica_groups=mesh['batch'=4,'centers'=8] {'centers'}, dimensions={0}, use_global_device_ids=true | all-gather | bytes 294912 | tf_op jit(solution)/shard_map/all_gather | solution.py:60
  68.6 8.9 %multiply_add_fusion = f32[512,512]{1,0:T(8,128)S(1)} fusion(f32[512,128]{1,0:T(8,128)S(1)} %all-gather, f32[512,128]{1,0:T(8,128)S(1)} %copy-done.3, f32[512]{0:T(512)S(1)} %multiply_add_fusion.1, f32[512]{0:T(512)S(1)} %multiply_add_fusion.2), kind=kOutput, calls=%fused_computation.11 | convolution fusion | flops 414187520 | bytes 1576960 | tf_op jit(solution)/shard_map/dot_general | solution.py:14
  77.5 1.8 fusion.8
  79.6 0.6 gather_fusion.1
  80.2 30.8 %all-gather.1 = f32[512,64]{1,0:T(8,128)S(1)} all-gather(f32[64,64]{1,0:T(8,128)S(1)} %gather_fusion.1), channel_id=3, replica_groups=mesh['batch'=4,'centers'=8] {'centers'}, dimensions={0}, use_global_device_ids=true | all-gather | bytes 147456 | tf_op jit(solution)/shard_map/all_gather | solution.py:63
  111.3 39.5 %all-reduce.5.cloned.1.call-done = f32[512,64]{0,1:T(8,128)} async-done(((f32[512,64]{0,1:T(8,128)}), f32[512,64]{0,1:T(8,128)}) %all-reduce.5.cloned.1.call-update) | async-done | bytes 131088 | tf_op jit(solution)/shard_map/psum | solution.py:64
  150.8 0.9 sub.36
  151.7 1.5 convolution_multiply_fusion.1
  153.3 31.3 %all-reduce.7.cloned.1.call-done = f32[512,64]{0,1:T(8,128)} async-done(((f32[512,64]{0,1:T(8,128)}), f32[512,64]{0,1:T(8,128)}) %all-reduce.7.cloned.1.call-update) | async-done | bytes 131088 | tf_op jit(solution)/shard_map/psum | solution.py:76
  184.6 1.0 copy.26
  185.6 0.7 gather_fusion.2
  186.5 12.2 %all_to_all.22 = f32[8,1,2048]{2,1,0:T(1,128)S(1)} all-to-all(f32[8,1,2048]{2,1,0:T(1,128)S(1)} %reshape.114), channel_id=1, replica_groups=mesh['batch'=4,'centers'=8] {'centers'}, dimensions={0} | all-to-all | bytes 131072 | tf_op jit(solution)/shard_map/all_to_all | solution.py:86
  199.2 0.8 reduce
  200.1 1.2 gather_fusion.3
  201.3 1.1 convolution_bitcast_fusion
  202.5 123.4 %all-reduce.9.cloned.1.call-done = f32[1024,64]{0,1:T(8,128)} async-done(((f32[1024,64]{0,1:T(8,128)}), f32[1024,64]{0,1:T(8,128)}) %all-reduce.9.cloned.1.call-update) | async-done | bytes 262160 | tf_op jit(solution)/shard_map/psum | solution.py:95
  325.9 1.6 convolution_bitcast_fusion.1
  327.7 6.9 %scatter_fusion.1 = f32[8,32,64]{2,1,0:T(8,128)S(1)} fusion(f32[8,32,64]{2,1,0:T(8,128)S(1)} %broadcast_in_dim.8, s32[128]{0:T(128)S(1)} %get-tuple-element.8, f32[128,64]{1,0:T(8,128)S(1)} %copy.27), kind=kCustom, calls=%fused_computation.5 | custom fusion | bytes 99328 | tf_op jit(solution)/shard_map/scatter | solution.py:103
  334.6 0.8 reshape.116
  335.3 4.5 %all-to-all-start.2 = ((f32[8,1,2048]{2,1,0:T(1,128)}), f32[8,1,2048]{2,1,0:T(1,128)S(1)}, u32[]{:S(2)}, u32[]{:S(2)}) async-start(f32[8,1,2048]{2,1,0:T(1,128)} %reshape.116), calls=%async_computation.2 | async-start | bytes 131072 | tf_op jit(solution)/shard_map/all_to_all | solution.py:105
  339.9 6.9 %all-to-all-done.2 = f32[8,1,2048]{2,1,0:T(1,128)S(1)} async-done(((f32[8,1,2048]{2,1,0:T(1,128)}), f32[8,1,2048]{2,1,0:T(1,128)S(1)}, u32[]{:S(2)}, u32[]{:S(2)}) %all-to-all-start.2) | async-done | bytes 65568 | tf_op jit(solution)/shard_map/all_to_all | solution.py:105
  346.7 0.8 reduce.1
  347.6 1.7 scatter_custom_fusion.2
  349.4 0.8 copy.28
  350.3 0.7 copy.29
  351.0 27.9 %all-reduce.11.cloned.1.call-done = f32[512,64]{0,1:T(8,128)} async-done(((f32[512,64]{0,1:T(8,128)}), f32[512,64]{0,1:T(8,128)}) %all-reduce.11.cloned.1.call-update) | async-done | bytes 131088 | tf_op jit(solution)/shard_map/psum | solution.py:107
  378.9 1.6 sub.38
  (50 shorter events, 2.5 us)
Async XLA Ops:
  7.2 194.2 %copy-start = (f32[128,1024]{1,0:T(8,128)S(1)}, f32[128,1024]{1,0:T(8,128)}, u32[]{:S(2)}) copy-start(f32[128,1024]{1,0:T(8,128)} %param.14) | copy-start | bytes 1572868
  7.2 0.7 copy-start.6
  8.3 0.7 copy-start.8
  9.0 27.4 %copy-start.3 = (f32[512,128]{1,0:T(8,128)S(1)}, f32[512,128]{1,0:T(8,128)}, u32[]{:S(2)}) copy-start(f32[512,128]{1,0:T(8,128)} %param.12) | copy-start | bytes 786436
  9.0 27.6 %copy-start.5 = (f32[1024,128]{1,0:T(8,128)S(1)}, f32[1024,128]{1,0:T(8,128)}, u32[]{:S(2)}) copy-start(f32[1024,128]{1,0:T(8,128)} %param.9) | copy-start | bytes 1572868
  28.9 7.5 %copy-start.9 = (s32[64]{0:T(128)S(1)}, s32[64]{0:T(128)}, u32[]{:S(2)}) copy-start(s32[64]{0:T(128)} %param.11) | copy-start | bytes 772
  28.9 82.3 %all-to-all-start = ((s32[8,1,32]{2,1,0:T(1,128)}), s32[8,1,32]{2,1,0:T(1,128)S(1)}, u32[]{:S(2)}, u32[]{:S(2)}) async-start(s32[8,1,32]{2,1,0:T(1,128)} %bitcast.4), calls=%async_computation | async-start | bytes 8192 | tf_op jit(solution)/shard_map/all_to_all | solution.py:84
  36.3 114.5 %all-reduce.5.cloned.1.call-start = ((), (), s32[]{:S(2)}) async-start(), calls=%async_computation.3 | async-start | bytes 262144 | tf_op jit(solution)/shard_map/psum | solution.py:64
  68.6 8.9 %copy-start.4 = (f32[512,64]{0,1:T(8,128)S(1)}, f32[512,64]{0,1:T(8,128)}, u32[]{:S(2)}) copy-start(f32[512,64]{0,1:T(8,128)} %param.13) | copy-start | bytes 393220
  77.5 1.9 copy-start.2
  79.4 105.2 %all-reduce.7.cloned.1.call-start = ((), (), s32[]{:S(2)}) async-start(), calls=%async_computation.4 | async-start | bytes 262144 | tf_op jit(solution)/shard_map/psum | solution.py:76
  153.2 172.7 %all-reduce.9.cloned.1.call-start = ((), (), s32[]{:S(2)}) async-start(), calls=%async_computation.5 | async-start | bytes 524288 | tf_op jit(solution)/shard_map/psum | solution.py:95
  202.5 123.4 %copy-start.7 = (f32[1024]{0:T(1024)S(1)}, f32[1024]{0:T(1024)}, u32[]{:S(2)}) copy-start(f32[1024]{0:T(1024)} %param.15) | copy-start | bytes 12292
  335.3 11.4 %all-to-all-start.2 = ((f32[8,1,2048]{2,1,0:T(1,128)}), f32[8,1,2048]{2,1,0:T(1,128)S(1)}, u32[]{:S(2)}, u32[]{:S(2)}) async-start(f32[8,1,2048]{2,1,0:T(1,128)} %reshape.116), calls=%async_computation.2 | async-start | bytes 131072 | tf_op jit(solution)/shard_map/all_to_all | solution.py:105
  339.8 39.0 %all-reduce.11.cloned.1.call-start = ((), (), s32[]{:S(2)}) async-start(), calls=%async_computation.6 | async-start | bytes 262144 | tf_op jit(solution)/shard_map/psum | solution.py:107
  350.1 28.7 %copy-start.1 = (f32[512,64]{0,1:T(8,128)S(1)}, f32[512,64]{0,1:T(8,128)}, u32[]{:S(2)}) copy-start(f32[512,64]{0,1:T(8,128)} %all-reduce.7.cloned.1.call-done) | copy-start | bytes 393220
Sparse Core Ops, SparseCore 0:
  79.5 71.2 all-reduce.4
  153.7 30.8 all-reduce.6
  202.6 123.2 all-reduce.8
  350.3 28.5 all-reduce.10
where the time goes:
time: 388 us; the launch traced here: 387 us
  waiting for transfers between devices  229 us (59%)
  blocking collectives  74.3 us (19%)
  local copies, waits for them, and re-layouts  36 us (9%)
  matrix products  14.9 us (4%)
  between operations  14 us (4%)
  starting transfers between devices  12.1 us (3%)
  other arithmetic  6.6 us (2%)
    psum x1, waiting for transfers between devices, per_device(): coeff = lax.psum(coeff_part, ('batch', 'centers'))  123 us
    psum x1, waiting for transfers between devices, per_device(): prediction = lax.psum(partial_pred, 'centers')  39.5 us
    psum x1, waiting for transfers between devices, per_device(): grads = lax.psum(grads_part, 'batch')  31.3 us
    all_gather x1, blocking collectives, per_device(): lax.all_gather(local_rows, 'centers', axis=0, tiled=True)  31.2 us
    all_gather x1, blocking collectives, per_device(): all_targets = lax.all_gather(local_targets, 'centers', axis=0, tiled=True)  30.8 us
    psum x1, waiting for transfers between devices, per_device(): correction = lax.psum(corr_part, 'batch')  27.9 us
    scatter x1, local copies, waits for them, and re-layouts, per_device(): jnp.zeros((group_size, slots), jnp.int32).at[owner, slot_rank]  19.9 us
    all_to_all x1, blocking collectives, per_device(): lax.all_to_all(found, 'centers', split_axis=0, concat_axis=0, tiled=True)  12.2 us
  transfers between devices with their start and end apart: 6, of which 5 were waited for; matrix products, arithmetic and copies ran while one was open for 3% of the time, Pallas kernels for 0%

commit v1 on v0

--- a/solution.py
+++ b/solution.py
@@ -92,7 +92,7 @@
         precision=highest,
         preferred_element_type=jnp.float32,
     )
-    coeff = lax.psum(coeff_part, ("batch", "centers"))
+    coeff = jnp.sum(lax.all_gather(coeff_part, ("batch", "centers")), axis=0)
     corr_rows = jnp.dot(
         eig_vectors,
         eig_scale[:, None] * coeff,

time: 388 us -> 323 us (0.83)
  waiting for transfers between devices: 229 us -> 153 us
  local copies, waits for them, and re-layouts: 36 us -> 44.4 us
    psum x1 -> x0, waiting for transfers between devices: 123 us -> none  [per_device(): coeff = lax.psum(coeff_part, ('batch', 'centers'))]
    all_gather x0 -> x1, waiting for transfers between devices: none -> 74.4 us  [per_device(): coeff = jnp.sum(lax.all_gather(coeff_part, ('batch', 'centers')), axis=0)]
    psum x1, waiting for transfers between devices: 39.5 us -> 12.8 us  [per_device(): prediction = lax.psum(partial_pred, 'centers')]
    unnamed x26 -> x21, local copies, waits for them, and re-layouts: 2.76 us -> 10.1 us
  transfers between devices with their start and end apart: 6 -> 6, of which waited for: 5 -> 5; matrix products, arithmetic and copies ran while one was open for 3% -> 7% of each run, Pallas kernels for 0% -> 0%
where the time goes in v1:
time: 323 us; the launch traced here: 322 us
  waiting for transfers between devices  153 us (47%)
  blocking collectives  76 us (24%)
  local copies, waits for them, and re-layouts  44.4 us (14%)
  matrix products  15 us (5%)
  between operations  14 us (4%)
  other arithmetic  9.73 us (3%)
  starting transfers between devices  9.72 us (3%)
    all_gather x1, waiting for transfers between devices, per_device(): coeff = jnp.sum(lax.all_gather(coeff_part, ('batch', 'centers')), axis=0)  74.4 us
    all_gather x1, blocking collectives, per_device(): lax.all_gather(local_rows, 'centers', axis=0, tiled=True)  32.6 us
    psum x1, waiting for transfers between devices, per_device(): grads = lax.psum(grads_part, 'batch')  31.3 us
    all_gather x1, blocking collectives, per_device(): all_targets = lax.all_gather(local_targets, 'centers', axis=0, tiled=True)  31.3 us
    psum x1, waiting for transfers between devices, per_device(): correction = lax.psum(corr_part, 'batch')  27.9 us
    scatter x1, local copies, waits for them, and re-layouts, per_device(): jnp.zeros((group_size, slots), jnp.int32).at[owner, slot_rank]  19.9 us
    psum x1, waiting for transfers between devices, per_device(): prediction = lax.psum(partial_pred, 'centers')  12.8 us
    all_to_all x1, blocking collectives, per_device(): lax.all_to_all(found, 'centers', split_axis=0, concat_axis=0, tiled=True)  12.2 us
  transfers between devices with their start and end apart: 6, of which 5 were waited for; matrix products, arithmetic and copies ran while one was open for 7% of the time, Pallas kernels for 0%

profile of v1, /device:TPU:0, one launch (start us, length us, event | category | flops | bytes accessed | tf_op | source)
XLA Modules:
  0.0 322.2 jit_solution(1715061193122446783)
XLA Ops:
  7.2 0.7 compare_select_fusion.3
  7.9 1.6 gather_fusion
  9.6 32.6 %all-gather = f32[512,128]{1,0:T(8,128)S(1)} all-gather(f32[64,128]{1,0:T(8,128)S(1)} %gather_fusion), channel_id=2, replica_groups=mesh['batch'=4,'centers'=8] {'centers'}, dimensions={0}, use_global_device_ids=true | all-gather | bytes 294912 | tf_op jit(solution)/shard_map/all_gather | solution.py:60
  42.3 1.1 multiply_reduce_fusion
  43.4 9.9 %multiply_add_fusion = f32[512,512]{1,0:T(8,128)S(1)} fusion(f32[512,128]{1,0:T(8,128)S(1)} %all-gather, f32[512,128]{1,0:T(8,128)} %param.12, f32[512]{0:T(512)S(1)} %multiply_add_fusion.1, f32[512]{0:T(512)S(1)} %multiply_add_fusion.2), kind=kOutput, calls=%fused_computation.12 | convolution fusion | flops 414187520 | bytes 1576960 | tf_op jit(solution)/shard_map/dot_general | solution.py:14
  53.4 1.8 fusion.8
  56.3 19.9 %scatter_fusion = s32[8,32]{1,0:T(8,128)} fusion(s32[8,32]{1,0:T(8,128)} %broadcast.104, s32[128]{0:T(128)S(1)} %get-tuple-element.8, s32[128]{0:T(128)S(1)} %copy-done.6), kind=kCustom, calls=%fused_computation.4 | custom fusion | bytes 2560 | tf_op jit(solution)/shard_map/scatter | solution.py:83
  76.1 5.6 %all-to-all-start = ((s32[8,1,32]{2,1,0:T(1,128)}), s32[8,1,32]{2,1,0:T(1,128)S(1)}, u32[]{:S(2)}, u32[]{:S(2)}) async-start(s32[8,1,32]{2,1,0:T(1,128)} %bitcast.4), calls=%async_computation | async-start | bytes 8192 | tf_op jit(solution)/shard_map/all_to_all | solution.py:84
  82.6 31.3 %all-gather.1 = f32[512,64]{1,0:T(8,128)S(1)} all-gather(f32[64,64]{1,0:T(8,128)S(1)} %gather_fusion.1), channel_id=3, replica_groups=mesh['batch'=4,'centers'=8] {'centers'}, dimensions={0}, use_global_device_ids=true | all-gather | bytes 147456 | tf_op jit(solution)/shard_map/all_gather | solution.py:63
  114.1 12.8 %all-reduce.4.cloned.1.call-done = f32[512,64]{0,1:T(8,128)} async-done(((f32[512,64]{0,1:T(8,128)}), f32[512,64]{0,1:T(8,128)}) %all-reduce.4.cloned.1.call-update) | async-done | bytes 131088 | tf_op jit(solution)/shard_map/psum | solution.py:64
  126.8 0.9 sub.36
  127.8 1.4 convolution_multiply_fusion.1
  129.3 31.3 %all-reduce.6.cloned.1.call-done = f32[512,64]{0,1:T(8,128)} async-done(((f32[512,64]{0,1:T(8,128)}), f32[512,64]{0,1:T(8,128)}) %all-reduce.6.cloned.1.call-update) | async-done | bytes 131088 | tf_op jit(solution)/shard_map/psum | solution.py:76
  160.6 1.0 copy.26
  161.7 0.7 gather_fusion.2
  162.5 12.2 %all_to_all.22 = f32[8,1,2048]{2,1,0:T(1,128)S(1)} all-to-all(f32[8,1,2048]{2,1,0:T(1,128)S(1)} %reshape.115), channel_id=1, replica_groups=mesh['batch'=4,'centers'=8] {'centers'}, dimensions={0} | all-to-all | bytes 131072 | tf_op jit(solution)/shard_map/all_to_all | solution.py:86
  175.2 0.8 reduce
  176.1 1.2 gather_fusion.3
  177.4 1.1 convolution_bitcast_fusion
  178.5 74.4 %all-gather.5.cloned.1.call-done = f32[32768,64]{0,1:T(8,128)} async-done(((f32[1024,64]{0,1:T(8,128)}), f32[32768,64]{0,1:T(8,128)}) %all-gather.5.cloned.1.call-update) | async-done | bytes 8388624 | tf_op jit(solution)/shard_map/all_gather | solution.py:95
  252.9 8.1 %copy.30 = f32[8,8,32,1024]{3,2,1,0:T(8,128)S(1)} copy(f32[8,8,32,1024]{3,1,2,0:T(8,128)} %bitcast.38) | data formatting | bytes 16777216
  261.1 1.5 bitcast_reduce_fusion
  263.4 6.9 %scatter_fusion.1 = f32[8,32,64]{2,1,0:T(8,128)S(1)} fusion(f32[8,32,64]{2,1,0:T(8,128)S(1)} %broadcast_in_dim.8, s32[128]{0:T(128)S(1)} %get-tuple-element.8, f32[128,64]{1,0:T(8,128)S(1)} %copy.27), kind=kCustom, calls=%fused_computation.5 | custom fusion | bytes 99328 | tf_op jit(solution)/shard_map/scatter | solution.py:103
  270.3 0.8 reshape.117
  271.0 4.0 %all-to-all-start.2 = ((f32[8,1,2048]{2,1,0:T(1,128)}), f32[8,1,2048]{2,1,0:T(1,128)S(1)}, u32[]{:S(2)}, u32[]{:S(2)}) async-start(f32[8,1,2048]{2,1,0:T(1,128)} %reshape.117), calls=%async_computation.2 | async-start | bytes 131072 | tf_op jit(solution)/shard_map/all_to_all | solution.py:105
  275.1 6.9 %all-to-all-done.2 = f32[8,1,2048]{2,1,0:T(1,128)S(1)} async-done(((f32[8,1,2048]{2,1,0:T(1,128)}), f32[8,1,2048]{2,1,0:T(1,128)S(1)}, u32[]{:S(2)}, u32[]{:S(2)}) %all-to-all-start.2) | async-done | bytes 65568 | tf_op jit(solution)/shard_map/all_to_all | solution.py:105
  281.9 0.8 reduce.1
  282.8 1.7 scatter_custom_fusion.2
  284.5 0.8 copy.28
  285.4 0.7 copy.29
  286.1 27.9 %all-reduce.8.cloned.1.call-done = f32[512,64]{0,1:T(8,128)} async-done(((f32[512,64]{0,1:T(8,128)}), f32[512,64]{0,1:T(8,128)}) %all-reduce.8.cloned.1.call-update) | async-done | bytes 131088 | tf_op jit(solution)/shard_map/psum | solution.py:107
  314.0 1.6 sub.38
  (46 shorter events, 4.1 us)
Async XLA Ops:
  7.2 170.2 %copy-start = (f32[128,1024]{1,0:T(8,128)S(1)}, f32[128,1024]{1,0:T(8,128)}, u32[]{:S(2)}) copy-start(f32[128,1024]{1,0:T(8,128)} %param.14) | copy-start | bytes 1572868
  7.2 119.6 %all-reduce.4.cloned.1.call-start = ((), (), s32[]{:S(2)}) async-start(), calls=%async_computation.3 | async-start | bytes 262144 | tf_op jit(solution)/shard_map/psum | solution.py:64
  43.4 10.0 %copy-start.3 = (f32[512,64]{0,1:T(8,128)S(1)}, f32[512,64]{0,1:T(8,128)}, u32[]{:S(2)}) copy-start(f32[512,64]{0,1:T(8,128)} %param.13) | copy-start | bytes 393220
  43.4 11.8 %copy-start.4 = (s32[128,1]{0,1:T(1,128)S(1)}, s32[128,1]{0,1:T(1,128)}, u32[]{:S(2)}) copy-start(s32[128,1]{0,1:T(1,128)} %param.16) | copy-start | bytes 1540
  43.4 12.9 %copy-start.6 = (s32[128]{0:T(128)S(1)}, s32[128]{0:T(128)}, u32[]{:S(2)}) copy-start(s32[128]{0:T(128)} %param.17) | copy-start | bytes 1540
  43.4 38.3 %copy-start.2 = (f32[1024,64]{0,1:T(8,128)S(1)}, f32[1024,64]{0,1:T(8,128)}, u32[]{:S(2)}) copy-start(f32[1024,64]{0,1:T(8,128)} %param.10) | copy-start | bytes 786436
  76.1 37.8 %all-to-all-start = ((s32[8,1,32]{2,1,0:T(1,128)}), s32[8,1,32]{2,1,0:T(1,128)S(1)}, u32[]{:S(2)}, u32[]{:S(2)}) async-start(s32[8,1,32]{2,1,0:T(1,128)} %bitcast.4), calls=%async_computation | async-start | bytes 8192 | tf_op jit(solution)/shard_map/all_to_all | solution.py:84
  81.7 78.9 %all-reduce.6.cloned.1.call-start = ((), (), s32[]{:S(2)}) async-start(), calls=%async_computation.4 | async-start | bytes 262144 | tf_op jit(solution)/shard_map/psum | solution.py:76
  129.2 123.7 %all-gather.5.cloned.1.call-start = ((), (), s32[]{:S(2)}) async-start(), calls=%async_computation.6 | async-start | bytes 8650752 | tf_op jit(solution)/shard_map/all_gather | solution.py:95
  261.0 1.5 copy-start.5
  261.1 53.0 %copy-start.1 = (f32[512,64]{0,1:T(8,128)S(1)}, f32[512,64]{0,1:T(8,128)}, u32[]{:S(2)}) copy-start(f32[512,64]{0,1:T(8,128)} %all-reduce.6.cloned.1.call-done) | copy-start | bytes 393220
  271.0 10.9 %all-to-all-start.2 = ((f32[8,1,2048]{2,1,0:T(1,128)}), f32[8,1,2048]{2,1,0:T(1,128)S(1)}, u32[]{:S(2)}, u32[]{:S(2)}) async-start(f32[8,1,2048]{2,1,0:T(1,128)} %reshape.117), calls=%async_computation.2 | async-start | bytes 131072 | tf_op jit(solution)/shard_map/all_to_all | solution.py:105
  275.0 39.0 %all-reduce.8.cloned.1.call-start = ((), (), s32[]{:S(2)}) async-start(), calls=%async_computation.5 | async-start | bytes 262144 | tf_op jit(solution)/shard_map/psum | solution.py:107
Sparse Core Ops, SparseCore 0:
  55.3 71.4 all-reduce.3
  129.7 30.8 all-reduce.5
  178.7 74.2 all-gather.4
  285.5 28.5 all-reduce.7
